TPU v7x, 32 devices: a whole 2x2x4 slice. The times are simulated.
32 devices in a mesh: dp: 2 (over x), layer: 4 (over y, core), tensor: 4 (over z).
Axes of the slice: x: 2, y: 2, z: 4, core: 2. Of those that a mesh axis runs over, the one named last changes fastest.
Arguments:
- embeddings: bfloat16 [256, 4096], P('dp', 'tensor'), may hold values from -180 to 180
- layer_weight: bfloat16 [8, 4096, 4096], P('layer', None, 'tensor'), may hold values from -0.09375 to 0.09375
- rotation: float32 [4096, 4096], P(('dp', 'layer'), 'tensor'), may hold values from -3.2 to 3.2
Outputs:
- updated_rotation: float32 [4096, 4096], P(('dp', 'layer'), 'tensor')
All inputs are finite; a program needn't handle non-finite values.
Results may differ from a plain program's by a relative error of at most 0.0042.
Values may be sent and summed in bfloat16 or wider, within the bound.
A program may use at most 128 MiB of HBM per device.

v0:
```python
import math
import jax
import jax.numpy as jnp
from jax import lax
from jax.sharding import PartitionSpec as P

D = 4096
MICRO = 4


def passed_along(value, axis, steps):
    count = lax.axis_size(axis)
    initial, last = (max(0, -steps), min(count, count - steps))
    return lax.ppermute(value, axis, [(source, source + steps) for source in range(initial, last)])


def normalize(hidden):
    widened = hidden.astype(jnp.float32)
    inverse = lax.rsqrt(jnp.mean(widened * widened, axis=-1, keepdims=True) + 1e-05)
    return (widened, (widened * inverse).astype(jnp.bfloat16))


def shards(embeddings, layer_weight, rotation):
    exact_mode = lax.Precision.HIGHEST
    root_width = math.sqrt(D)
    rotated = rotation / root_width
    panel = lax.all_gather(rotated, ("dp", "layer"), axis=0, tiled=True)
    section = lax.axis_index("layer")
    width = embeddings.shape[1]
    full_width = width * lax.axis_size("tensor")
    column_start = lax.axis_index("tensor") * width
    micro_rows = embeddings.shape[0] // MICRO
    section_layers = layer_weight.shape[0]
    steps_total = MICRO + lax.axis_size("layer") - 1

    def join_columns(shard):
        return lax.all_gather(shard, "tensor", axis=1, tiled=True)

    def run_section(hidden):
        records = []
        shard = None
        for level in range(section_layers):
            widened, normed = normalize(hidden)
            update = jnp.dot(normed, layer_weight[level], preferred_element_type=jnp.float32)
            own_part = lax.dynamic_slice_in_dim(widened, column_start, width, 1)
            shard = (own_part + update).astype(jnp.bfloat16)
            records.append(normed)
            if level + 1 < section_layers:
                hidden = join_columns(shard)
        return (shard, jnp.stack(records))

    def step_fn(step, carry):
        previous, records_all = carry
        position = step - section
        valid = (position >= 0) & (position < MICRO)
        slot_index = jnp.clip(position, 0, MICRO - 1)
        fresh = lax.dynamic_slice_in_dim(embeddings, slot_index * micro_rows, micro_rows, 0)
        incoming = jnp.where(section == 0, join_columns(fresh), previous)
        shard, records = run_section(incoming)
        current = lax.dynamic_slice_in_dim(records_all, slot_index, 1, 1)
        chosen = jnp.where(valid, records[:, None], current)
        records_all = lax.dynamic_update_slice_in_dim(records_all, chosen, slot_index, 1)
        passed = passed_along(join_columns(shard), "layer", 1)
        return (passed, records_all)

    start_state = jnp.zeros((micro_rows, full_width), jnp.bfloat16)
    records_zero = jnp.zeros((section_layers, MICRO, micro_rows, full_width), jnp.bfloat16)
    final_state, records_all = lax.fori_loop(0, steps_total, step_fn, (start_state, records_zero))
    activations = records_all.reshape(-1, full_width)
    projected = jnp.dot(activations.astype(jnp.float32), panel, precision=exact_mode)
    cubed = projected * projected * projected
    columns = activations.astype(jnp.float32)
    summed = lax.psum_scatter(
        lax.dot_general(columns, cubed, (((0,), (0,)), ((), ())), precision=exact_mode),
        ("dp", "layer"),
        scatter_dimension=0,
        tiled=True,
    )
    gradient = summed / (embeddings.shape[0] * lax.axis_size("dp"))
    cross = lax.dot_general(gradient, panel, (((1,), (1,)), ((), ())), precision=exact_mode)
    cross_rows = lax.psum(cross, "tensor")
    swapped = lax.all_to_all(cross_rows, ("dp", "layer"), split_axis=1, concat_axis=0, tiled=True)
    skew_rows = cross_rows - swapped.T
    square_total = lax.psum(jnp.sum(skew_rows * skew_rows), ("dp", "layer"))
    mean_square = square_total / (full_width * full_width)
    step_size = 0.5 / jnp.sqrt(full_width * (mean_square + 1e-06))
    first_product = jnp.dot(skew_rows, panel, precision=exact_mode)
    first_guess = rotated - step_size * first_product
    second_product = jnp.dot(
        skew_rows,
        lax.all_gather(first_guess, ("dp", "layer"), axis=0, tiled=True),
        precision=exact_mode,
    )
    refined = rotated - 0.5 * step_size * (first_product + second_product)
    return root_width * refined


def solution(mesh):
    return jax.shard_map(
        shards,
        mesh=mesh,
        in_specs=(P("dp", "tensor"), P("layer", None, "tensor"), P(("dp", "layer"), "tensor")),
        out_specs=P(("dp", "layer"), "tensor"),
        check_vma=False,
    )
```

profile of v0, /device:TPU:0, one launch (start us, length us, event | category | flops | bytes accessed | tf_op | source)
XLA Modules:
  0.0 1216.2 jit_solution(3677848573825620444)
XLA Ops:
  10.1 428.7 %while.17 = (s32[]{:T(128)}, bf16[32,4096]{1,0:T(8,128)(2,1)S(1)}, bf16[2,4,32,4096]{3,2,1,0:T(8,128)(2,1)S(1)}, pred[]{:T(512)}, s32[]{:T(128)}, /*index=5*/bf1...) while((s32[]{:T(128)}, bf16[32,4096]{1,0:T(8,128)(2,1)S(1)}, ...), condition=%wide.region_3.4_spmd, body=%wide.region_0.3_spmd.sunk | while | flops 541065280 | bytes 26151456 | solution.py:68
  11.0 15.6 %all_gather.38 = bf16[32,4096]{1,0:T(8,128)(2,1)S(1)} all-gather(bf16[32,1024]{1,0:T(8,128)(2,1)S(1)} %constant_dynamic-slice_fusion.4), channel_id=1, replica_groups=mesh['dp'=2,'layer'=4,'tensor'=4] {'tensor'}, dimensions={1}, use_global_device_ids=true | all-gather | bytes 327680 | tf_op jit(solution)/shard_map/while/body/eval_jaxpr/all_gather | solution.py:37
  31.9 14.4 %all_gather.39 = bf16[32,4096]{1,0:T(8,128)(2,1)S(1)} all-gather(bf16[32,1024]{1,0:T(8,128)(2,1)S(1)} %fusion.45), channel_id=1, replica_groups=mesh['dp'=2,'layer'=4,'tensor'=4] {'tensor'}, dimensions={1}, use_global_device_ids=true | all-gather | bytes 327680 | tf_op jit(solution)/shard_map/while/body/eval_jaxpr/all_gather | solution.py:37
  46.5 5.0 fusion.46
  51.5 15.1 %all_gather.40 = bf16[32,4096]{1,0:T(8,128)(2,1)} all-gather(bf16[32,1024]{1,0:T(8,128)(2,1)S(1)} %fusion.46), channel_id=1, replica_groups=mesh['dp'=2,'layer'=4,'tensor'=4] {'tensor'}, dimensions={1}, use_global_device_ids=true | all-gather | bytes 327680 | tf_op jit(solution)/shard_map/while/body/eval_jaxpr/all_gather | solution.py:37
  70.2 13.9 %all_gather.38 = bf16[32,4096]{1,0:T(8,128)(2,1)S(1)} all-gather(bf16[32,1024]{1,0:T(8,128)(2,1)S(1)} %constant_dynamic-slice_fusion.4), channel_id=1, replica_groups=mesh['dp'=2,'layer'=4,'tensor'=4] {'tensor'}, dimensions={1}, use_global_device_ids=true | all-gather | bytes 327680 | tf_op jit(solution)/shard_map/while/body/eval_jaxpr/all_gather | solution.py:37
  84.4 5.0 fusion.45
  89.4 13.9 %all_gather.39 = bf16[32,4096]{1,0:T(8,128)(2,1)S(1)} all-gather(bf16[32,1024]{1,0:T(8,128)(2,1)S(1)} %fusion.45), channel_id=1, replica_groups=mesh['dp'=2,'layer'=4,'tensor'=4] {'tensor'}, dimensions={1}, use_global_device_ids=true | all-gather | bytes 327680 | tf_op jit(solution)/shard_map/while/body/eval_jaxpr/all_gather | solution.py:37
  103.5 5.0 fusion.46
  108.5 15.2 %all_gather.40 = bf16[32,4096]{1,0:T(8,128)(2,1)} all-gather(bf16[32,1024]{1,0:T(8,128)(2,1)S(1)} %fusion.46), channel_id=1, replica_groups=mesh['dp'=2,'layer'=4,'tensor'=4] {'tensor'}, dimensions={1}, use_global_device_ids=true | all-gather | bytes 327680 | tf_op jit(solution)/shard_map/while/body/eval_jaxpr/all_gather | solution.py:37
  129.2 13.9 %all_gather.38 = bf16[32,4096]{1,0:T(8,128)(2,1)S(1)} all-gather(bf16[32,1024]{1,0:T(8,128)(2,1)S(1)} %constant_dynamic-slice_fusion.4), channel_id=1, replica_groups=mesh['dp'=2,'layer'=4,'tensor'=4] {'tensor'}, dimensions={1}, use_global_device_ids=true | all-gather | bytes 327680 | tf_op jit(solution)/shard_map/while/body/eval_jaxpr/all_gather | solution.py:37
  143.3 5.0 fusion.45
  148.3 14.0 %all_gather.39 = bf16[32,4096]{1,0:T(8,128)(2,1)S(1)} all-gather(bf16[32,1024]{1,0:T(8,128)(2,1)S(1)} %fusion.45), channel_id=1, replica_groups=mesh['dp'=2,'layer'=4,'tensor'=4] {'tensor'}, dimensions={1}, use_global_device_ids=true | all-gather | bytes 327680 | tf_op jit(solution)/shard_map/while/body/eval_jaxpr/all_gather | solution.py:37
  162.5 5.0 fusion.46
  167.5 14.6 %all_gather.40 = bf16[32,4096]{1,0:T(8,128)(2,1)} all-gather(bf16[32,1024]{1,0:T(8,128)(2,1)S(1)} %fusion.46), channel_id=1, replica_groups=mesh['dp'=2,'layer'=4,'tensor'=4] {'tensor'}, dimensions={1}, use_global_device_ids=true | all-gather | bytes 327680 | tf_op jit(solution)/shard_map/while/body/eval_jaxpr/all_gather | solution.py:37
  182.2 7.4 collective-permute-start
  191.7 13.8 %all_gather.38 = bf16[32,4096]{1,0:T(8,128)(2,1)S(1)} all-gather(bf16[32,1024]{1,0:T(8,128)(2,1)S(1)} %constant_dynamic-slice_fusion.4), channel_id=1, replica_groups=mesh['dp'=2,'layer'=4,'tensor'=4] {'tensor'}, dimensions={1}, use_global_device_ids=true | all-gather | bytes 327680 | tf_op jit(solution)/shard_map/while/body/eval_jaxpr/all_gather | solution.py:37
  205.8 5.0 fusion.45
  210.8 13.8 %all_gather.39 = bf16[32,4096]{1,0:T(8,128)(2,1)S(1)} all-gather(bf16[32,1024]{1,0:T(8,128)(2,1)S(1)} %fusion.45), channel_id=1, replica_groups=mesh['dp'=2,'layer'=4,'tensor'=4] {'tensor'}, dimensions={1}, use_global_device_ids=true | all-gather | bytes 327680 | tf_op jit(solution)/shard_map/while/body/eval_jaxpr/all_gather | solution.py:37
  229.8 14.5 %all_gather.40 = bf16[32,4096]{1,0:T(8,128)(2,1)} all-gather(bf16[32,1024]{1,0:T(8,128)(2,1)S(1)} %fusion.46), channel_id=1, replica_groups=mesh['dp'=2,'layer'=4,'tensor'=4] {'tensor'}, dimensions={1}, use_global_device_ids=true | all-gather | bytes 327680 | tf_op jit(solution)/shard_map/while/body/eval_jaxpr/all_gather | solution.py:37
  244.3 6.7 collective-permute-start
  253.2 13.8 %all_gather.38 = bf16[32,4096]{1,0:T(8,128)(2,1)S(1)} all-gather(bf16[32,1024]{1,0:T(8,128)(2,1)S(1)} %constant_dynamic-slice_fusion.4), channel_id=1, replica_groups=mesh['dp'=2,'layer'=4,'tensor'=4] {'tensor'}, dimensions={1}, use_global_device_ids=true | all-gather | bytes 327680 | tf_op jit(solution)/shard_map/while/body/eval_jaxpr/all_gather | solution.py:37
  272.2 13.8 %all_gather.39 = bf16[32,4096]{1,0:T(8,128)(2,1)S(1)} all-gather(bf16[32,1024]{1,0:T(8,128)(2,1)S(1)} %fusion.45), channel_id=1, replica_groups=mesh['dp'=2,'layer'=4,'tensor'=4] {'tensor'}, dimensions={1}, use_global_device_ids=true | all-gather | bytes 327680 | tf_op jit(solution)/shard_map/while/body/eval_jaxpr/all_gather | solution.py:37
  291.3 14.5 %all_gather.40 = bf16[32,4096]{1,0:T(8,128)(2,1)} all-gather(bf16[32,1024]{1,0:T(8,128)(2,1)S(1)} %fusion.46), channel_id=1, replica_groups=mesh['dp'=2,'layer'=4,'tensor'=4] {'tensor'}, dimensions={1}, use_global_device_ids=true | all-gather | bytes 327680 | tf_op jit(solution)/shard_map/while/body/eval_jaxpr/all_gather | solution.py:37
  305.8 7.3 collective-permute-start
  315.3 13.9 %all_gather.38 = bf16[32,4096]{1,0:T(8,128)(2,1)S(1)} all-gather(bf16[32,1024]{1,0:T(8,128)(2,1)S(1)} %constant_dynamic-slice_fusion.4), channel_id=1, replica_groups=mesh['dp'=2,'layer'=4,'tensor'=4] {'tensor'}, dimensions={1}, use_global_device_ids=true | all-gather | bytes 327680 | tf_op jit(solution)/shard_map/while/body/eval_jaxpr/all_gather | solution.py:37
  329.5 5.0 fusion.45
  334.5 13.8 %all_gather.39 = bf16[32,4096]{1,0:T(8,128)(2,1)S(1)} all-gather(bf16[32,1024]{1,0:T(8,128)(2,1)S(1)} %fusion.45), channel_id=1, replica_groups=mesh['dp'=2,'layer'=4,'tensor'=4] {'tensor'}, dimensions={1}, use_global_device_ids=true | all-gather | bytes 327680 | tf_op jit(solution)/shard_map/while/body/eval_jaxpr/all_gather | solution.py:37
  348.5 5.0 fusion.46
  353.5 14.5 %all_gather.40 = bf16[32,4096]{1,0:T(8,128)(2,1)} all-gather(bf16[32,1024]{1,0:T(8,128)(2,1)S(1)} %fusion.46), channel_id=1, replica_groups=mesh['dp'=2,'layer'=4,'tensor'=4] {'tensor'}, dimensions={1}, use_global_device_ids=true | all-gather | bytes 327680 | tf_op jit(solution)/shard_map/while/body/eval_jaxpr/all_gather | solution.py:37
  368.1 7.2 collective-permute-start
  377.5 13.9 %all_gather.38 = bf16[32,4096]{1,0:T(8,128)(2,1)S(1)} all-gather(bf16[32,1024]{1,0:T(8,128)(2,1)S(1)} %constant_dynamic-slice_fusion.4), channel_id=1, replica_groups=mesh['dp'=2,'layer'=4,'tensor'=4] {'tensor'}, dimensions={1}, use_global_device_ids=true | all-gather | bytes 327680 | tf_op jit(solution)/shard_map/while/body/eval_jaxpr/all_gather | solution.py:37
  396.7 13.8 %all_gather.39 = bf16[32,4096]{1,0:T(8,128)(2,1)S(1)} all-gather(bf16[32,1024]{1,0:T(8,128)(2,1)S(1)} %fusion.45), channel_id=1, replica_groups=mesh['dp'=2,'layer'=4,'tensor'=4] {'tensor'}, dimensions={1}, use_global_device_ids=true | all-gather | bytes 327680 | tf_op jit(solution)/shard_map/while/body/eval_jaxpr/all_gather | solution.py:37
  415.7 14.5 %all_gather.40 = bf16[32,4096]{1,0:T(8,128)(2,1)} all-gather(bf16[32,1024]{1,0:T(8,128)(2,1)S(1)} %fusion.46), channel_id=1, replica_groups=mesh['dp'=2,'layer'=4,'tensor'=4] {'tensor'}, dimensions={1}, use_global_device_ids=true | all-gather | bytes 327680 | tf_op jit(solution)/shard_map/while/body/eval_jaxpr/all_gather | solution.py:37
  430.2 7.2 collective-permute-start
  438.8 12.0 fusion.29
  450.8 10.4 fusion.25
  461.4 131.6 %reduce-scatter.2.cloned.1.call-done = f32[512,1024]{1,0:T(8,128)} async-done(((f32[4096,1024]{1,0:T(8,128)}), f32[512,1024]{1,0:T(8,128)}) %reduce-scatter.2.cloned.1.call-update) | async-done | bytes 2097168 | tf_op jit(solution)/shard_map/reduce_scatter | solution.py:73
  593.0 31.8 %fusion.23 = f32[512,4096]{1,0:T(8,128)} fusion(f32[4096,1024]{1,0:T(8,128)} %all-gather.3.cloned.1.call-done, f32[512,1024]{1,0:T(8,128)} %reduce-scatter.2.cloned.1.call-done), kind=kOutput, calls=%fused_computation.29 | convolution fusion | flops 25770328064 | bytes 27262976 | tf_op jit(solution)/shard_map/dot_general | solution.py:80
  624.9 290.9 %all-reduce.2.cloned.1.call-done = f32[512,4096]{1,0:T(8,128)} async-done(((f32[512,4096]{1,0:T(8,128)}), f32[512,4096]{1,0:T(8,128)}) %all-reduce.2.cloned.1.call-update) | async-done | bytes 8388624 | tf_op jit(solution)/shard_map/psum | solution.py:81
  915.8 9.0 copy.10
  924.8 100.4 %all_to_all.19 = f32[512,8,512]{0,2,1:T(8,128)} all-to-all(f32[512,8,512]{0,2,1:T(8,128)} %bitcast.73), channel_id=1, replica_groups=mesh['dp'=2,'layer'=4,'tensor'=4] {'dp','layer'}, dimensions={1} | all-to-all | bytes 16777216 | tf_op jit(solution)/shard_map/all_to_all | solution.py:82
  1025.2 8.2 copy.14
  1033.4 6.3 multiply_reduce_fusion.2
  1039.7 13.2 %psum.15 = f32[]{:T(128)} all-reduce(f32[]{:T(128)} %multiply_reduce_fusion.2), channel_id=1, replica_groups=mesh['dp'=2,'layer'=4,'tensor'=4] {'dp','layer'}, use_global_device_ids=true, to_apply=%region_7.8 | all-reduce | flops 1 | bytes 8 | tf_op jit(solution)/shard_map/psum | solution.py:84
  1053.6 33.4 %multiply_subtract_fusion = (f32[512,1024]{1,0:T(8,128)}, f32[512,1024]{1,0:T(8,128)}) fusion(f32[]{:T(128)S(6)} %div.29, f32[512,1024]{1,0:T(8,128)S(1)} %copy-done, f32[4096,1024]{1,0:T(8,128)} %all-gather.3.cloned.1.call-done, f32[512,4096]{1,0:T(8,128)} %all-reduce.2.cloned.1.call-done, f32[4096,512]{0,1:T(8,128)} %bitcast.68), kind=kOutput, calls=%fused_computation.28 | convolution fusion | flops 25773473792 | bytes 39845892 | tf_op jit(solution)/shard_map/dot_general | solution.py:87
  1087.0 88.1 %all-gather.5.cloned.1.call-done = f32[4096,1024]{1,0:T(8,128)} async-done(((f32[512,1024]{1,0:T(8,128)}), f32[4096,1024]{1,0:T(8,128)}) %all-gather.5.cloned.1.call-update) | async-done | bytes 16777232 | tf_op jit(solution)/shard_map/all_gather | solution.py:91
  1175.1 34.5 %subtract_multiply_fusion = f32[512,1024]{1,0:T(8,128)} fusion(f32[512,1024]{1,0:T(8,128)} %get-tuple-element.203, f32[4096,1024]{1,0:T(8,128)} %all-gather.5.cloned.1.call-done, f32[]{:T(128)S(6)} %mul.119, f32[512,1024]{1,0:T(8,128)S(1)} %copy-done, f32[512,4096]{1,0:T(8,128)} %all-reduce.2.cloned.1.call-done, f32[4096,512]{0,1:T(8,128)} %bitcast.69), kind=kOutput, calls=%fused_computation.27 | convolution fusion | flops 25774522368 | bytes 39845892 | tf_op jit(solution)/shard_map/dot_general | solution.py:89
  (111 shorter events, 56.7 us)
Async XLA Ops:
  6.5 432.3 %all-gather.3.cloned.1.call-start = ((), (), s32[]{:S(2)}) async-start(), calls=%async_computation.2 | async-start | bytes 18874368 | tf_op jit(solution)/shard_map/all_gather | solution.py:27
  9.8 583.2 %reduce-scatter.2.cloned.1.call-start = ((), (), s32[]{:S(2)}) async-start(), calls=%async_computation.3 | async-start | bytes 18874368 | tf_op jit(solution)/shard_map/reduce_scatter | solution.py:73
  66.7 2.7 collective-permute-start
  123.7 4.6 collective-permute-start
  182.2 8.7 collective-permute-start
  244.3 8.0 collective-permute-start
  305.8 8.7 collective-permute-start
  368.1 8.6 collective-permute-start
  430.2 8.6 collective-permute-start
  461.2 454.6 %all-reduce.2.cloned.1.call-start = ((), (), s32[]{:S(2)}) async-start(), calls=%async_computation.4 | async-start | bytes 16777216 | tf_op jit(solution)/shard_map/psum | solution.py:81
  624.8 550.3 %all-gather.5.cloned.1.call-start = ((), (), s32[]{:S(2)}) async-start(), calls=%async_computation.5 | async-start | bytes 18874368 | tf_op jit(solution)/shard_map/all_gather | solution.py:91
  924.8 108.6 %slice-start = ((s8[8388608]{0:T(1024)(128)(4,1)}), s8[4194304]{0:T(1024)(128)(4,1)S(1)}, s32[]{:S(2)}) async-start(s8[8388608]{0:T(1024)(128)(4,1)} %bitcast.65), calls=%async_computation.6 | async-start | bytes 8388608
  1025.2 8.2 slice-start.1
  1033.4 20.2 %copy-start = (f32[512,1024]{1,0:T(8,128)S(1)}, f32[512,1024]{1,0:T(8,128)}, u32[]{:S(2)}) copy-start(f32[512,1024]{1,0:T(8,128)} %param.7) | copy-start | bytes 6291460
Sparse Core Ops, SparseCore 0:
  9.9 92.6 all-gather.2
  461.3 131.6 reduce-scatter.1
  625.0 290.8 all-reduce.1
  1087.1 87.9 all-gather.4
where the time goes:
time: 1220 us
  waiting for transfers between devices  517 us (42%)
  blocking collectives  413 us (34%)
  matrix products  192 us (16%)
  starting transfers between devices  40.8 us (3%)
  local copies, waits for them, and re-layouts  23.7 us (2%)
  other arithmetic  15.3 us (1%)
  between operations  13.9 us (1%)
    all_gather x21, blocking collectives, join_columns(): return lax.all_gather(shard, 'tensor', axis=1, tiled=True)  299 us
    psum x1, waiting for transfers between devices, shards(): cross_rows = lax.psum(cross, 'tensor')  291 us
    reduce_scatter x1, waiting for transfers between devices, shards(): lax.psum_scatter(lax.dot_general(columns, cubed, (((0,), (0,)), ((), ()))...  132 us
    all_to_all x1, blocking collectives, shards(): lax.all_to_all(cross_rows, ('dp', 'layer'), split_axis=1, concat_axis=0,...  100 us
    all_gather x1, waiting for transfers between devices, shards(): lax.all_gather(first_guess, ('dp', 'layer'), axis=0, tiled=True)  88.1 us
    dot_general x14, matrix products, run_section(): jnp.dot(normed, layer_weight[level], preferred_element_type=jnp.float32)  69.8 us
    ppermute x7, starting transfers between devices, passed_along(): lax.ppermute(value, axis, [(source, source + steps) for source in range(i...  40.5 us
    dot_general x1, matrix products, shards(): jnp.dot(skew_rows, lax.all_gather(first_guess, ('dp', 'layer'), axis=0, t...  34.5 us
  transfers between devices with their start and end apart: 11, of which 10 were waited for; matrix products, arithmetic and copies ran while one was open for 7% of the time, Pallas kernels for 0%

commit v1 on v0

--- a/solution.py
+++ b/solution.py
@@ -34,7 +34,26 @@
     steps_total = MICRO + lax.axis_size("layer") - 1
 
     def join_columns(shard):
-        return lax.all_gather(shard, "tensor", axis=1, tiled=True)
+
+        def lay_layers_all(frame, comm_axis, which_dim):
+            extent = lax.axis_size(comm_axis)
+            rack = list(map(lambda i: (i, (i + 1) % extent), range(extent)))
+            q_next = range(extent)
+            kept_rows = list(map(lambda i: (i, (i - 1) % extent), q_next))
+            y2, shaped = ([frame], [frame])
+            for _ in range(extent // 2):
+                all_rows = lax.ppermute(y2[-1], comm_axis, rack)
+                y2.append(all_rows)
+            for _ in [*range((extent - 1) // 2)]:
+                shaped.append(lax.ppermute(shaped[-1], axis_name=comm_axis, perm=kept_rows))
+            e_next = jnp.concatenate([*y2[::-1], *shaped[1:]], which_dim)
+            return jnp.roll(
+                e_next,
+                (lax.axis_index(comm_axis) - extent // 2) * frame.shape[which_dim],
+                which_dim,
+            )
+
+        return lay_layers_all(shard, "tensor", 1)
 
     def run_section(hidden):
         records = []

time: 1220 us -> 1190 us (0.975)
  blocking collectives: 413 us -> 114 us
  waiting for transfers between devices: 517 us -> 688 us
  starting transfers between devices: 40.8 us -> 122 us
  other arithmetic: 15.3 us -> 30.6 us
    all_gather x21 -> x0, blocking collectives: 299 us -> none  [join_columns(): return lax.all_gather(shard, 'tensor', axis=1, tiled=True)]
    ppermute x0 -> x63, waiting for transfers between devices: none -> 176 us  [the longest x42 175 us: lay_layers_all(): all_rows = lax.ppermute(y2[-1], comm_axis, rack)]
    ppermute x0 -> x63, starting transfers between devices: none -> 82.6 us  [the longest x21 78.7 us: lay_layers_all(): shaped.append(lax.ppermute(shaped[-1], axis_name=comm_axis, perm=kept_rows))]
  transfers between devices with their start and end apart: 11 -> 74, of which waited for: 10 -> 53; matrix products, arithmetic and copies ran while one was open for 7% -> 8% of each run, Pallas kernels for 0% -> 0%
where the time goes in v1:
time: 1190 us
  waiting for transfers between devices  688 us (58%)
  matrix products  193 us (16%)
  starting transfers between devices  122 us (10%)
  blocking collectives  114 us (10%)
  other arithmetic  30.6 us (3%)
  local copies, waits for them, and re-layouts  23.6 us (2%)
  between operations  14.1 us (1%)
    psum x1, waiting for transfers between devices, shards(): cross_rows = lax.psum(cross, 'tensor')  291 us
    ppermute x42, waiting for transfers between devices, lay_layers_all(): all_rows = lax.ppermute(y2[-1], comm_axis, rack)  175 us
    reduce_scatter x1, waiting for transfers between devices, shards(): lax.psum_scatter(lax.dot_general(columns, cubed, (((0,), (0,)), ((), ()))...  126 us
    all_to_all x1, blocking collectives, shards(): lax.all_to_all(cross_rows, ('dp', 'layer'), split_axis=1, concat_axis=0,...  101 us
    all_gather x1, waiting for transfers between devices, shards(): lax.all_gather(first_guess, ('dp', 'layer'), axis=0, tiled=True)  88.1 us
    ppermute x21, starting transfers between devices, lay_layers_all(): shaped.append(lax.ppermute(shaped[-1], axis_name=comm_axis, perm=kept_rows))  78.7 us
    dot_general x14, matrix products, run_section(): jnp.dot(normed, layer_weight[level], preferred_element_type=jnp.float32)  69.9 us
    ppermute x7, starting transfers between devices, passed_along(): lax.ppermute(value, axis, [(source, source + steps) for source in range(i...  39.8 us
  transfers between devices with their start and end apart: 74, of which 53 were waited for; matrix products, arithmetic and copies ran while one was open for 8% of the time, Pallas kernels for 0%

profile of v1, /device:TPU:0, one launch (start us, length us, event | category | flops | bytes accessed | tf_op | source)
XLA Modules:
  0.0 1185.8 jit_solution(18088958684086828137)
XLA Ops:
  10.1 402.8 %while.17 = (s32[]{:T(128)}, bf16[32,4096]{1,0:T(8,128)(2,1)S(1)}, bf16[2,4,32,4096]{3,2,1,0:T(8,128)(2,1)S(1)}, pred[]{:T(512)}, s32[]{:T(128)}, /*index=5*/bf1...) while((s32[]{:T(128)}, bf16[32,4096]{1,0:T(8,128)(2,1)S(1)}, ...), condition=%wide.region_3.5_spmd, body=%wide.region_0.4_spmd.sunk | while | flops 546439296 | bytes 28315532 | solution.py:87
  19.0 5.5 collective-permute-done.2
  36.6 6.0 collective-permute-done.5
  43.5 5.0 fusion.73
  55.4 5.9 collective-permute-done.7
  71.5 6.2 collective-permute-done.2
  89.8 6.1 collective-permute-done.5
  96.8 5.0 fusion.73
  108.1 5.9 collective-permute-done.7
  127.8 6.1 collective-permute-done.2
  134.8 5.0 fusion.72
  146.0 6.1 collective-permute-done.5
  153.1 5.0 fusion.73
  164.3 6.0 collective-permute-done.7
  171.1 7.3 collective-permute-start.9
  186.5 6.1 collective-permute-done.2
  193.5 5.0 fusion.72
  204.6 6.0 collective-permute-done.5
  222.8 6.3 collective-permute-done.7
  230.0 7.0 collective-permute-start.9
  245.0 6.1 collective-permute-done.2
  252.0 5.0 fusion.72
  263.1 6.0 collective-permute-done.5
  281.3 6.6 collective-permute-done.7
  288.8 6.9 collective-permute-start.9
  303.7 6.1 collective-permute-done.2
  310.7 5.0 fusion.72
  321.9 6.1 collective-permute-done.5
  328.9 5.0 fusion.73
  340.1 6.6 collective-permute-done.7
  347.5 6.0 collective-permute-start.9
  361.6 6.1 collective-permute-done.2
  379.8 6.0 collective-permute-done.5
  398.0 6.6 collective-permute-done.7
  405.4 6.4 collective-permute-start.9
  412.9 12.0 %fusion.55 = f32[256,1024]{1,0:T(8,128)S(1)} fusion(bf16[256,4096]{1,0:T(8,128)(2,1)S(1)} %bitcast.70, f32[4096,1024]{1,0:T(8,128)} %all-gather.3.cloned.1.call-done), kind=kOutput, calls=%fused_computation.84 | convolution fusion | flops 12884901888 | bytes 19922944 | tf_op jit(solution)/shard_map/dot_general | solution.py:89
  424.9 10.9 fusion.49
  435.8 126.4 %reduce-scatter.2.cloned.1.call-done = f32[512,1024]{1,0:T(8,128)} async-done(((f32[4096,1024]{1,0:T(8,128)}), f32[512,1024]{1,0:T(8,128)}) %reduce-scatter.2.cloned.1.call-update) | async-done | bytes 2097168 | tf_op jit(solution)/shard_map/reduce_scatter | solution.py:92
  562.2 31.8 %fusion.47 = f32[512,4096]{1,0:T(8,128)} fusion(f32[4096,1024]{1,0:T(8,128)} %all-gather.3.cloned.1.call-done, f32[512,1024]{1,0:T(8,128)} %reduce-scatter.2.cloned.1.call-done), kind=kOutput, calls=%fused_computation.76 | convolution fusion | flops 25770328064 | bytes 27262976 | tf_op jit(solution)/shard_map/dot_general | solution.py:99
  594.1 290.9 %all-reduce.2.cloned.1.call-done = f32[512,4096]{1,0:T(8,128)} async-done(((f32[512,4096]{1,0:T(8,128)}), f32[512,4096]{1,0:T(8,128)}) %all-reduce.2.cloned.1.call-update) | async-done | bytes 8388624 | tf_op jit(solution)/shard_map/psum | solution.py:100
  885.0 9.0 copy.10
  894.1 100.6 %all_to_all.19 = f32[512,8,512]{0,2,1:T(8,128)} all-to-all(f32[512,8,512]{0,2,1:T(8,128)} %bitcast.73), channel_id=1, replica_groups=mesh['dp'=2,'layer'=4,'tensor'=4] {'dp','layer'}, dimensions={1} | all-to-all | bytes 16777216 | tf_op jit(solution)/shard_map/all_to_all | solution.py:101
  994.6 8.2 copy.14
  1002.9 6.3 multiply_reduce_fusion.2
  1009.2 13.0 %psum.15 = f32[]{:T(128)} all-reduce(f32[]{:T(128)} %multiply_reduce_fusion.2), channel_id=1, replica_groups=mesh['dp'=2,'layer'=4,'tensor'=4] {'dp','layer'}, use_global_device_ids=true, to_apply=%region_7.9 | all-reduce | flops 1 | bytes 8 | tf_op jit(solution)/shard_map/psum | solution.py:103
  1022.8 33.4 %multiply_subtract_fusion = (f32[512,1024]{1,0:T(8,128)}, f32[512,1024]{1,0:T(8,128)}) fusion(f32[]{:T(128)S(6)} %div.29, f32[512,1024]{1,0:T(8,128)S(1)} %copy-done, f32[4096,1024]{1,0:T(8,128)} %all-gather.3.cloned.1.call-done, f32[512,4096]{1,0:T(8,128)} %all-reduce.2.cloned.1.call-done, f32[4096,512]{0,1:T(8,128)} %bitcast.68), kind=kOutput, calls=%fused_computation.75 | convolution fusion | flops 25773473792 | bytes 39845892 | tf_op jit(solution)/shard_map/dot_general | solution.py:106
  1056.2 88.1 %all-gather.5.cloned.1.call-done = f32[4096,1024]{1,0:T(8,128)} async-done(((f32[512,1024]{1,0:T(8,128)}), f32[4096,1024]{1,0:T(8,128)}) %all-gather.5.cloned.1.call-update) | async-done | bytes 16777232 | tf_op jit(solution)/shard_map/all_gather | solution.py:110
  1144.4 34.7 %subtract_multiply_fusion = f32[512,1024]{1,0:T(8,128)} fusion(f32[512,1024]{1,0:T(8,128)} %get-tuple-element.214, f32[4096,1024]{1,0:T(8,128)} %all-gather.5.cloned.1.call-done, f32[]{:T(128)S(6)} %mul.138, f32[512,1024]{1,0:T(8,128)S(1)} %copy-done, f32[512,4096]{1,0:T(8,128)} %all-reduce.2.cloned.1.call-done, f32[4096,512]{0,1:T(8,128)} %bitcast.69), kind=kOutput, calls=%fused_computation.74 | convolution fusion | flops 25774522368 | bytes 39845892 | tf_op jit(solution)/shard_map/dot_general | solution.py:108
  (209 shorter events, 203.9 us)
Async XLA Ops:
  6.5 406.4 %all-gather.3.cloned.1.call-start = ((), (), s32[]{:S(2)}) async-start(), calls=%async_computation.2 | async-start | bytes 18874368 | tf_op jit(solution)/shard_map/all_gather | solution.py:27
  9.8 552.5 %reduce-scatter.2.cloned.1.call-start = ((), (), s32[]{:S(2)}) async-start(), calls=%async_computation.3 | async-start | bytes 18874368 | tf_op jit(solution)/shard_map/reduce_scatter | solution.py:92
  11.0 7.4 collective-permute-start.1
  30.4 6.1 collective-permute-start.4
  30.5 6.1 collective-permute-start.3
  48.5 6.8 collective-permute-start.6
  48.7 6.7 collective-permute-start.8
  65.5 6.1 collective-permute-start
  71.5 6.2 collective-permute-start.2
  83.6 6.1 collective-permute-start.4
  83.7 6.1 collective-permute-start.3
  89.7 6.2 collective-permute-start.5
  101.8 6.1 collective-permute-start.6
  114.8 6.1 collective-permute-start.9
  121.8 6.1 collective-permute-start
  139.8 6.1 collective-permute-start.4
  139.9 6.1 collective-permute-start.3
  146.0 6.2 collective-permute-start.5
  158.1 6.1 collective-permute-start.6
  164.2 6.1 collective-permute-start.7
  171.1 8.4 collective-permute-start.9
  198.5 6.1 collective-permute-start.4
  198.5 6.1 collective-permute-start.3
  204.6 6.1 collective-permute-start.5
  216.6 6.1 collective-permute-start.6
  222.7 6.5 collective-permute-start.7
  230.0 8.1 collective-permute-start.9
  257.0 6.1 collective-permute-start.4
  257.0 6.1 collective-permute-start.3
  263.1 6.1 collective-permute-start.5
  275.1 6.1 collective-permute-start.6
  281.2 6.8 collective-permute-start.7
  288.8 8.0 collective-permute-start.9
  303.7 6.1 collective-permute-start.2
  315.7 6.1 collective-permute-start.4
  315.8 6.1 collective-permute-start.3
  321.8 6.1 collective-permute-start.5
  333.9 6.1 collective-permute-start.6
  340.0 6.7 collective-permute-start.7
  347.5 7.1 collective-permute-start.9
  373.6 6.1 collective-permute-start.4
  373.6 6.1 collective-permute-start.3
  379.7 6.1 collective-permute-start.5
  391.7 6.1 collective-permute-start.6
  397.8 6.8 collective-permute-start.7
  405.4 7.5 collective-permute-start.9
  435.8 449.3 %all-reduce.2.cloned.1.call-start = ((), (), s32[]{:S(2)}) async-start(), calls=%async_computation.4 | async-start | bytes 16777216 | tf_op jit(solution)/shard_map/psum | solution.py:100
  594.1 550.3 %all-gather.5.cloned.1.call-start = ((), (), s32[]{:S(2)}) async-start(), calls=%async_computation.5 | async-start | bytes 18874368 | tf_op jit(solution)/shard_map/all_gather | solution.py:110
  (29 other events, 289.9 us)
Sparse Core Ops, SparseCore 0:
  9.9 92.5 all-gather.2
  435.9 126.2 reduce-scatter.1
  594.2 290.8 all-reduce.1
  1056.4 87.9 all-gather.4
